TPU v7x, 256 devices: a whole 4x4x8 slice. The times are simulated.
256 devices in a mesh: star: 8 (over x, core), row: 32 (over z, y).
Axes of the slice: x: 4, y: 4, z: 8, core: 2. Of those that a mesh axis runs over, the one named last changes fastest.
Arguments:
- feature_maps: bfloat16 [64, 1024, 1024], P(None, 'row'), may hold values from -6 to 6
- coef_table: bfloat16 [64, 64], replicated, may hold values from -0.119628906 to 0.119628906
- star_counts: int32 [8], replicated, may hold values from 1 to 12, 32 in all
- star_cells: int32 [8, 12], replicated, may hold values from 0 to 63
- star_bands: int32 [8, 12], replicated, may hold values from 0 to 7
- psf_cotangent: bfloat16 [96, 1024, 1024], P('star', 'row'), may hold values from -6 to 6
Outputs:
- map_grad: float32 [64, 1024, 1024], P('star', 'row')
- coef_grad: float32 [64, 64], replicated
Inputs may be any that keep to these rules, and one draw needn't show every extreme that they name: The live stars of group g fill its slots 0 to star_counts[g] - 1; the counts sum to 32, and some group has exactly 12.
All inputs are finite; a program needn't handle non-finite values.
Results may differ from a plain program's by a relative error of at most 0.008.
Values may be sent and summed in bfloat16 or wider, within the bound.
No kernel may reach another device: no remote copies, remote signals or barrier semaphores. Data moves between devices by JAX's collectives and lax.ppermute only.
A program may use at most 128 MiB of HBM per device.

v0:
```python
import jax
import jax.numpy as jnp
from jax import lax
from jax.sharding import PartitionSpec as P

BANDS = 8


def fourier_tables(pupil_size):
    index_row = jnp.arange(pupil_size, dtype=jnp.int32)
    products = index_row[:, None] * index_row[None, :] % pupil_size
    angles = 2.0 * jnp.pi / pupil_size * products.astype(jnp.float32)
    return (jnp.cos(angles).astype(jnp.bfloat16), (-jnp.sin(angles)).astype(jnp.bfloat16))


def aperture_rows(first_row, row_count, pupil_size):
    centre = 0.5 * (pupil_size - 1)
    row_pos = (first_row + jnp.arange(row_count, dtype=jnp.int32)).astype(jnp.float32) - centre
    col_pos = jnp.arange(pupil_size, dtype=jnp.int32).astype(jnp.float32) - centre
    radius = row_pos[:, None] * row_pos[:, None] + col_pos[None, :] * col_pos[None, :]
    return jnp.where(radius <= 0.25 * pupil_size * pupil_size, 1.0, 0.0).astype(jnp.float32)


def wave_numbers(band_ids):
    wavelength = 0.55 + 0.35 * band_ids.astype(jnp.float32) / (BANDS - 1)
    return 2.0 * jnp.pi / wavelength


def table_pick(values, indices):
    positions = jnp.arange(values.shape[0], dtype=jnp.int32)
    chosen = jnp.where(positions[None, :] == indices[:, None], values[None, :], 0)
    return jnp.sum(chosen, axis=1)


def per_device(feature_maps, coef_table, star_counts, star_cells, star_bands, psf_cotangent):
    groups = lax.axis_size("star")
    my_group = lax.axis_index("star")
    slot_count = psf_cotangent.shape[0]
    map_count, row_count, pupil_size = feature_maps.shape
    flat_cells = star_cells.reshape(-1)
    flat_bands = star_bands.reshape(-1)
    cell_count = coef_table.shape[0]
    within = jnp.arange(slot_count, dtype=jnp.int32)
    owner_group = jnp.zeros_like(within) + my_group
    live_mask = within < table_pick(star_counts, owner_group)
    owner_group, within, live_mask = (owner_group, within, live_mask)
    slot_index = owner_group * slot_count + within
    cell_ids = table_pick(flat_cells, slot_index)
    band_ids = table_pick(flat_bands, slot_index)
    cell_hot = cell_ids[:, None] == jnp.arange(cell_count, dtype=jnp.int32)[None, :]
    coef_rows = jnp.dot(
        cell_hot.astype(jnp.bfloat16), coef_table, preferred_element_type=jnp.float32
    ).astype(jnp.bfloat16)
    flat_maps = feature_maps.reshape(map_count, row_count * pupil_size)
    path_error = jnp.dot(coef_rows, flat_maps, preferred_element_type=jnp.float32).reshape(
        -1, row_count, pupil_size
    )
    wave_number = wave_numbers(band_ids)
    phase_angle = wave_number[:, None, None] * path_error
    aperture = aperture_rows(lax.axis_index("row") * row_count, row_count, pupil_size)
    cos_phase = jnp.cos(phase_angle)
    sin_phase = jnp.sin(phase_angle)
    pupil_field = jnp.stack([aperture * cos_phase, aperture * sin_phase], 1).astype(jnp.bfloat16)
    cos_table, sin_table = fourier_tables(pupil_size)
    inverse = 1.0 / pupil_size
    along_cos = jnp.einsum(
        "sarc,cv->sarv", pupil_field, cos_table, preferred_element_type=jnp.float32
    )
    along_sin = jnp.einsum(
        "sarc,cv->sarv", pupil_field, sin_table, preferred_element_type=jnp.float32
    )
    column_field = jnp.stack(
        [along_cos[:, 0] - along_sin[:, 1], along_sin[:, 0] + along_cos[:, 1]], 1
    ).astype(jnp.bfloat16)
    pieces = lax.all_to_all(column_field, "row", split_axis=3, concat_axis=2, tiled=True)
    row_cos = jnp.einsum("sarv,ru->savu", pieces, cos_table, preferred_element_type=jnp.float32)
    row_sin = jnp.einsum("sarv,ru->savu", pieces, sin_table, preferred_element_type=jnp.float32)
    real_part = (row_cos[:, 0] - row_sin[:, 1]) * inverse
    imag_part = (row_sin[:, 0] + row_cos[:, 1]) * inverse
    focal_field = jnp.stack([real_part, imag_part], 1)
    weight = jnp.where(live_mask, 2.0, 0.0).astype(jnp.float32)[:, None, None, None]
    focal_grad = (weight * psf_cotangent.astype(jnp.float32)[:, None] * focal_field).astype(
        jnp.bfloat16
    )
    back_cos = jnp.einsum(
        "savu,ur->savr", focal_grad, cos_table, preferred_element_type=jnp.float32
    )
    back_sin = jnp.einsum(
        "savu,ur->savr", focal_grad, sin_table, preferred_element_type=jnp.float32
    )
    spectrum_grad = jnp.stack(
        [(back_cos[:, 0] + back_sin[:, 1]) * inverse, (back_cos[:, 1] - back_sin[:, 0]) * inverse],
        1,
    ).astype(jnp.bfloat16)
    pieces = lax.all_to_all(spectrum_grad, "row", split_axis=3, concat_axis=2, tiled=True)
    col_cos = jnp.einsum("savr,vc->sarc", pieces, cos_table, preferred_element_type=jnp.float32)
    col_sin = jnp.einsum("savr,vc->sarc", pieces, sin_table, preferred_element_type=jnp.float32)
    pupil_grad = jnp.stack([col_cos[:, 0] + col_sin[:, 1], col_cos[:, 1] - col_sin[:, 0]], 1)
    phase_grad = aperture * (cos_phase * pupil_grad[:, 1] - sin_phase * pupil_grad[:, 0])
    path_grad = (
        (wave_number[:, None, None] * phase_grad)
        .astype(jnp.bfloat16)
        .reshape(-1, row_count * pupil_size)
    )
    map_scores = lax.dot_general(
        path_grad, flat_maps, (((1,), (1,)), ((), ())), preferred_element_type=jnp.float32
    )
    coef_part = lax.dot_general(
        cell_hot.astype(jnp.float32),
        map_scores * (1.0 / (8 * pupil_size)),
        (((0,), (0,)), ((), ())),
        precision=lax.Precision.HIGHEST,
    )
    coef_grad = lax.psum(coef_part, ("star", "row"))
    share = map_count // groups
    map_grad = lax.psum_scatter(
        lax.dot_general(
            coef_rows, path_grad, (((0,), (0,)), ((), ())), preferred_element_type=jnp.float32
        ),
        "star",
        scatter_dimension=0,
        tiled=True,
    )
    return (map_grad.reshape(share, row_count, pupil_size), coef_grad)


def solution(mesh):
    placed = (P(None, "row", None), P(), P(), P(), P(), P("star", "row", None))
    return jax.shard_map(
        per_device,
        mesh=mesh,
        in_specs=placed,
        out_specs=(P("star", "row", None), P()),
        check_vma=False,
    )
```

profile of v0, /device:TPU:1, one launch (start us, length us, event | category | flops | bytes accessed | tf_op | source)
XLA Modules:
  0.0 501.8 jit_solution(5607141360308045111)
XLA Ops:
  7.2 0.0 copy-start
  7.2 0.8 broadcast_in_dim.72
  8.0 0.8 broadcast_in_dim.75
  8.7 0.2 select_reduce_fusion
  9.0 0.0 copy-done
  9.0 0.2 convolution_convert_fusion
  9.2 6.7 %fusion.3 = f32[12,32,1024]{2,0,1:T(8,128)S(1)} fusion(bf16[12,64]{1,0:T(8,128)(2,1)S(1)} %convolution_convert_fusion, bf16[8,8,32,1024]{3,2,1,0:T(8,128)(2,1)} %bitcast.95), kind=kOutput, calls=%fused_computation.8 | convolution fusion | flops 50331648 | bytes 5768704 | tf_op jit(solution)/shard_map/dot_general | solution.py:55
  15.9 0.1 fusion.56
  16.0 8.4 %fusion.54 = (bf16[12,1,32,1024]{3,0,2,1:T(8,128)(2,1)S(1)}, bf16[12,1,32,1024]{3,0,2,1:T(8,128)(2,1)S(1)}) fusion(f32[12,32,1024]{2,0,1:T(8,128)S(1)} %fusion.3, f32[32,1024]{1,0:T(8,128)S(1)} %fusion.56, f32[12]{0:T(128)S(1)} %add_divide_fusion), kind=kLoop, calls=%fused_computation.67 | loop fusion | flops 1966080 | bytes 3276848 | tf_op jit(solution)/shard_map/stack | solution.py:63
  24.4 0.3 pad_maximum_fusion
  24.7 17.9 %fusion.28 = f32[12,2,32,1024]{3,2,1,0:T(8,128)S(1)} fusion(bf16[12,2,32,1024]{3,0,2,1:T(8,128)(2,1)S(1)} %pad_maximum_fusion), kind=kOutput, calls=%fused_computation.36 | convolution fusion | flops 1627389952 | bytes 4718592 | tf_op jit(solution)/shard_map/sarc,cv->sarv/dot_general | solution.py:69
  42.5 17.3 %fusion.36 = f32[12,2,32,1024]{3,2,1,0:T(8,128)S(1)} fusion(bf16[12,2,32,1024]{3,0,2,1:T(8,128)(2,1)S(1)} %pad_maximum_fusion), kind=kOutput, calls=%fused_computation.40 | convolution fusion | flops 1626341376 | bytes 4718592 | tf_op jit(solution)/shard_map/sarc,cv->sarv/dot_general | solution.py:66
  59.9 1.2 fusion.45
  61.1 1.3 pad_maximum_fusion.1
  62.4 15.1 %copy.45 = bf16[12,2,32,1024]{2,1,0,3:T(2,128)(2,1)} copy(bf16[12,2,32,1024]{3,2,1,0:T(8,128)(2,1)} %pad_maximum_fusion.1) | data formatting | bytes 3145728 | tf_op jit(solution)/shard_map/stack | solution.py:72
  77.5 13.8 %reshape.93 = bf16[32,2,12288]{2,1,0:T(2,128)(2,1)} reshape(bf16[1024,12,2,32]{3,2,1,0:T(2,128)(2,1)} %bitcast.93) | data formatting | bytes 3145728
  91.3 0.0 copy-start.6
  91.3 0.0 copy-start.5
  91.3 12.3 %all-to-all-start = ((bf16[32,2,12288]{2,1,0:T(2,128)(2,1)}), bf16[32,2,12288]{2,1,0:T(2,128)(2,1)}, u32[]{:S(2)}, u32[]{:S(2)}) async-start(bf16[32,2,12288]{2,1,0:T(2,128)(2,1)} %reshape.93), calls=%async_computation | async-start | bytes 3145728 | tf_op jit(solution)/shard_map/all_to_all | solution.py:75
  103.6 0.0 reduce-scatter.2.cloned.1.call-start
  103.7 0.0 copy-done.6
  103.7 0.1 select_reduce_fusion.2
  103.8 0.0 copy-done.5
  103.8 1.4 convert_multiply_fusion
  105.2 36.3 %all-to-all-done = bf16[32,2,12288]{2,1,0:T(2,128)(2,1)} async-done(((bf16[32,2,12288]{2,1,0:T(2,128)(2,1)}), bf16[32,2,12288]{2,1,0:T(2,128)(2,1)}, u32[]{:S(2)}, u32[]{:S(2)}) %all-to-all-start) | async-done | bytes 1572896 | tf_op jit(solution)/shard_map/all_to_all | solution.py:75
  141.5 14.3 %reshape.94 = bf16[1024,12,2,32]{3,2,1,0:T(2,128)(2,1)} reshape(bf16[32,2,12288]{2,1,0:T(2,128)(2,1)} %all-to-all-done) | data formatting | bytes 3145728
  155.7 9.5 %copy.107 = bf16[12,2,32,32,32]{2,3,4,1,0:T(8,128)(2,1)} copy(bf16[12,2,32,32,32]{2,1,0,4,3:T(2,128)(2,1)} %bitcast.89) | data formatting | bytes 3145728 | tf_op jit(solution)/shard_map/all_to_all | solution.py:75
  165.2 9.8 %all_to_all.29 = bf16[12,2,1024,32]{2,3,1,0:T(8,128)(2,1)} reshape(bf16[12,2,32,32,32]{3,2,4,1,0:T(8,128)(2,1)} %bitcast.90) | data formatting | bytes 3145728 | tf_op jit(solution)/shard_map/all_to_all | solution.py:75
  175.0 0.0 copy-start.3
  175.0 18.3 %fusion.26 = f32[12,2,32,1024]{3,2,1,0:T(8,128)S(1)} fusion(bf16[12,2,1024,32]{2,3,1,0:T(8,128)(2,1)} %all_to_all.29), kind=kOutput, calls=%fused_computation.35 | convolution fusion | flops 1627389952 | bytes 4718592 | tf_op jit(solution)/shard_map/sarv,ru->savu/dot_general | solution.py:77
  193.3 0.0 copy-done.3
  193.3 17.4 %fusion.34 = f32[12,2,32,1024]{3,2,1,0:T(8,128)S(1)} fusion(bf16[12,2,1024,32]{2,3,1,0:T(8,128)(2,1)S(1)} %copy-done.3), kind=kOutput, calls=%fused_computation.39 | convolution fusion | flops 1626341376 | bytes 4718592 | tf_op jit(solution)/shard_map/sarv,ru->savu/dot_general | solution.py:76
  210.7 0.0 copy-start.2
  210.7 1.0 fusion.43
  211.7 0.4 copy-done.2
  212.1 16.4 %fusion.32 = f32[12,2,32,1024]{3,2,1,0:T(8,128)S(1)} fusion(f32[12,1,32,1024]{3,2,1,0:T(8,128)S(1)} %get-tuple-element.15, f32[12,1,32,1024]{3,2,1,0:T(8,128)S(1)} %get-tuple-element.14, f32[12,32,1024]{2,1,0:T(8,128)S(1)} %copy-done.2), kind=kOutput, calls=%fused_computation.38 | convolution fusion | flops 1628700672 | bytes 7864320 | tf_op jit(solution)/shard_map/savu,ur->savr/dot_general | solution.py:85
  228.5 16.7 %fusion.24 = f32[12,2,32,1024]{3,2,1,0:T(8,128)S(1)} fusion(f32[12,1,32,1024]{3,2,1,0:T(8,128)S(1)} %get-tuple-element.15, f32[12,1,32,1024]{3,2,1,0:T(8,128)S(1)} %get-tuple-element.14, f32[12,32,1024]{2,1,0:T(8,128)S(1)} %copy-done.2), kind=kOutput, calls=%fused_computation.34 | convolution fusion | flops 1629749248 | bytes 7864320 | tf_op jit(solution)/shard_map/savu,ur->savr/dot_general | solution.py:88
  245.2 0.8 fusion.41
  246.0 1.3 pad_maximum_fusion.2
  247.2 15.1 %copy.47 = bf16[12,2,32,1024]{2,1,0,3:T(2,128)(2,1)} copy(bf16[12,2,32,1024]{3,2,1,0:T(8,128)(2,1)} %pad_maximum_fusion.2) | data formatting | bytes 3145728 | tf_op jit(solution)/shard_map/stack | solution.py:91
  262.3 14.2 %reshape.95 = bf16[32,2,12288]{2,1,0:T(2,128)(2,1)} reshape(bf16[1024,12,2,32]{3,2,1,0:T(2,128)(2,1)} %bitcast.94) | data formatting | bytes 3145728
  276.5 42.9 %all_to_all.36 = bf16[32,2,12288]{2,1,0:T(2,128)(2,1)} all-to-all(bf16[32,2,12288]{2,1,0:T(2,128)(2,1)} %reshape.95), channel_id=1, replica_groups=mesh['star'=8,'row'=32] {'row'}, dimensions={0} | all-to-all | bytes 3145728 | tf_op jit(solution)/shard_map/all_to_all | solution.py:95
  319.5 14.3 %reshape.96 = bf16[1024,12,2,32]{3,2,1,0:T(2,128)(2,1)} reshape(bf16[32,2,12288]{2,1,0:T(2,128)(2,1)} %all_to_all.36) | data formatting | bytes 3145728
  333.7 9.5 %copy.106 = bf16[12,2,32,32,32]{2,3,4,1,0:T(8,128)(2,1)} copy(bf16[12,2,32,32,32]{2,1,0,4,3:T(2,128)(2,1)} %bitcast.91) | data formatting | bytes 3145728 | tf_op jit(solution)/shard_map/all_to_all | solution.py:95
  343.2 9.8 %all_to_all.33 = bf16[12,2,1024,32]{2,3,1,0:T(8,128)(2,1)} reshape(bf16[12,2,32,32,32]{3,2,4,1,0:T(8,128)(2,1)} %bitcast.92) | data formatting | bytes 3145728 | tf_op jit(solution)/shard_map/all_to_all | solution.py:95
  353.0 0.0 copy-start.4
  353.0 18.3 %fusion.22 = f32[12,2,32,1024]{3,2,1,0:T(8,128)S(1)} fusion(bf16[12,2,1024,32]{2,3,1,0:T(8,128)(2,1)} %all_to_all.33), kind=kOutput, calls=%fused_computation.33 | convolution fusion | flops 1627389952 | bytes 4718592 | tf_op jit(solution)/shard_map/savr,vc->sarc/dot_general | solution.py:97
  371.3 0.0 copy-done.4
  371.3 17.0 %fusion.30 = f32[12,2,32,1024]{3,2,1,0:T(8,128)S(1)} fusion(bf16[12,2,1024,32]{2,3,1,0:T(8,128)(2,1)S(1)} %copy-done.4), kind=kOutput, calls=%fused_computation.37 | convolution fusion | flops 1626341376 | bytes 4718592 | tf_op jit(solution)/shard_map/savr,vc->sarc/dot_general | solution.py:96
  388.3 1.1 fusion.95
  389.4 11.4 %fusion.19 = bf16[12,32,1024]{2,0,1:T(8,128)(2,1)S(1)} fusion(f32[12,1,32,1024]{3,2,1,0:T(8,128)S(1)} %get-tuple-element.24, f32[12,1,32,1024]{3,2,1,0:T(8,128)S(1)} %get-tuple-element.19, f32[12,1,32,1024]{3,2,1,0:T(8,128)S(1)} %get-tuple-element.25, f32[12,1,32,1024]{3,2,1,0:T(8,128)S(1)} %get-tuple-element.18, f32[12,32,1024]{2,0,1:T(8,128)S(1)} %fusion.3, ...), kind=kLoop, calls=%fused_computation.29 | loop fusion | flops 3538944 | bytes 8781872 | tf_op jit(solution)/shard_map/convert_element_type | solution.py:102
  400.8 0.4 copy.53
  401.2 0.1 pad.8
  401.4 0.6 copy.64
  402.0 4.5 fusion.97
  406.5 0.0 reduce-scatter.2.cloned.1.call-update
  406.5 0.0 copy-start.1
  406.5 6.8 %fusion.51 = f32[12,64]{1,0:T(8,128)S(1)} fusion(bf16[12,32,1024]{2,0,1:T(8,128)(2,1)S(1)} %fusion.19, bf16[64,32,1024]{2,1,0:T(8,128)(2,1)} %param.6), kind=kOutput, calls=%fused_computation.65 | convolution fusion | flops 50332416 | bytes 4983808 | tf_op jit(solution)/shard_map/dot_general | solution.py:105
  413.3 0.3 fusion.57
  413.6 78.1 %psum.7 = f32[64,64]{1,0:T(8,128)} all-reduce(f32[64,64]{1,0:T(8,128)S(1)} %fusion.57), channel_id=1, replica_groups=mesh['star'=8,'row'=32] {'star','row'}, use_global_device_ids=true, to_apply=%region_4.5 | all-reduce | flops 4096 | bytes 32768 | tf_op jit(solution)/shard_map/psum | solution.py:114
  491.7 0.0 reduce-scatter.2.cloned.1.call-done
  491.7 2.8 copy.55
  494.5 0.0 copy-done.1
  (5 shorter events, 0.0 us)
Async XLA Ops:
  7.2 1.8 copy-start
  91.3 12.3 %copy-start.6 = (s32[8]{0:T(128)S(1)}, s32[8]{0:T(128)}, u32[]{:S(2)}) copy-start(s32[8]{0:T(128)} %param.8) | copy-start | bytes 100
  91.3 12.4 %copy-start.5 = (bf16[12,32,1024]{2,1,0:T(8,128)(2,1)S(1)}, bf16[12,32,1024]{2,1,0:T(8,128)(2,1)}, u32[]{:S(2)}) copy-start(bf16[12,32,1024]{2,1,0:T(8,128)(2,1)} %param.11) | copy-start | bytes 2359300
  91.3 50.2 %all-to-all-start = ((bf16[32,2,12288]{2,1,0:T(2,128)(2,1)}), bf16[32,2,12288]{2,1,0:T(2,128)(2,1)}, u32[]{:S(2)}, u32[]{:S(2)}) async-start(bf16[32,2,12288]{2,1,0:T(2,128)(2,1)} %reshape.93), calls=%async_computation | async-start | bytes 3145728 | tf_op jit(solution)/shard_map/all_to_all | solution.py:75
  103.6 388.1 %reduce-scatter.2.cloned.1.call-start = ((), (), s32[]{:S(2)}) async-start(), calls=%async_computation.3 | async-start | bytes 9437184 | tf_op jit(solution)/shard_map/reduce_scatter | solution.py:116
  175.0 18.3 %copy-start.3 = (bf16[12,2,1024,32]{2,3,1,0:T(8,128)(2,1)S(1)}, bf16[12,2,1024,32]{2,3,1,0:T(8,128)(2,1)}, u32[]{:S(2)}) copy-start(bf16[12,2,1024,32]{2,3,1,0:T(8,128)(2,1)} %all_to_all.29) | copy-start | bytes 4718596
  210.7 1.4 copy-start.2
  353.0 18.3 %copy-start.4 = (bf16[12,2,1024,32]{2,3,1,0:T(8,128)(2,1)S(1)}, bf16[12,2,1024,32]{2,3,1,0:T(8,128)(2,1)}, u32[]{:S(2)}) copy-start(bf16[12,2,1024,32]{2,3,1,0:T(8,128)(2,1)} %all_to_all.33) | copy-start | bytes 4718596
  406.5 88.0 %copy-start.1 = (bf16[64,64]{1,0:T(8,128)(2,1)S(1)}, bf16[64,64]{1,0:T(8,128)(2,1)}, u32[]{:S(2)}) copy-start(bf16[64,64]{1,0:T(8,128)(2,1)} %param.7) | copy-start | bytes 24580
Sparse Core Ops, SparseCore 0:
  406.6 54.6 reduce-scatter.1
where the time goes:
time: 509 us; the launch traced here: 502 us
  matrix products  158 us (31%)
  local copies, waits for them, and re-layouts  132 us (26%)
  blocking collectives  121 us (24%)
  waiting for transfers between devices  36.3 us (7%)
  other arithmetic  27.5 us (5%)
  between operations  14.7 us (3%)
  starting transfers between devices  12.3 us (2%)
    psum x1, blocking collectives, per_device(): coef_grad = lax.psum(coef_part, ('star', 'row'))  78.1 us
    unnamed x21, local copies, waits for them, and re-layouts  60.5 us
    all_to_all x1, blocking collectives, per_device(): lax.all_to_all(spectrum_grad, 'row', split_axis=3, concat_axis=2, tiled=T...  42.9 us
    all_to_all x1, waiting for transfers between devices, per_device(): lax.all_to_all(column_field, 'row', split_axis=3, concat_axis=2, tiled=True)  36.3 us
    all_to_all x2, local copies, waits for them, and re-layouts, per_device(): lax.all_to_all(column_field, 'row', split_axis=3, concat_axis=2, tiled=True)  19.3 us
    all_to_all x2, local copies, waits for them, and re-layouts, per_device(): lax.all_to_all(spectrum_grad, 'row', split_axis=3, concat_axis=2, tiled=T...  19.3 us
    dot_general x1, matrix products, per_device(): jnp.einsum('savr,vc->sarc', pieces, sin_table, preferred_element_type=jnp...  18.3 us
    dot_general x1, matrix products, per_device(): jnp.einsum('sarv,ru->savu', pieces, sin_table, preferred_element_type=jnp...  18.3 us
  transfers between devices with their start and end apart: 2, of which 1 were waited for; matrix products, arithmetic and copies ran while one was open for 2% of the time, Pallas kernels for 0%

commit v1 on v0

--- a/solution.py
+++ b/solution.py
@@ -4,6 +4,18 @@
 from jax.sharding import PartitionSpec as P
 
 BANDS = 8
+
+
+def update_the_sites(slab_in):
+    return jnp.concatenate(
+        lax.all_to_all(
+            jnp.stack(jnp.split(slab_in, lax.psum(1, axis_name="row"), axis=3)),
+            "row",
+            split_axis=0,
+            concat_axis=0,
+        ),
+        axis=2,
+    )
 
 
 def fourier_tables(pupil_size):
@@ -92,7 +104,7 @@
         [(back_cos[:, 0] + back_sin[:, 1]) * inverse, (back_cos[:, 1] - back_sin[:, 0]) * inverse],
         1,
     ).astype(jnp.bfloat16)
-    pieces = lax.all_to_all(spectrum_grad, "row", split_axis=3, concat_axis=2, tiled=True)
+    pieces = update_the_sites(spectrum_grad)
     col_cos = jnp.einsum("savr,vc->sarc", pieces, cos_table, preferred_element_type=jnp.float32)
     col_sin = jnp.einsum("savr,vc->sarc", pieces, sin_table, preferred_element_type=jnp.float32)
     pupil_grad = jnp.stack([col_cos[:, 0] + col_sin[:, 1], col_cos[:, 1] - col_sin[:, 0]], 1)

time: 509 us -> 486 us (0.955)
  local copies, waits for them, and re-layouts: 132 us -> 90.2 us
  other arithmetic: 27.5 us -> 50 us
    unnamed x0 -> x31, other arithmetic: none -> 24.5 us
    unnamed x21 -> x17, local copies, waits for them, and re-layouts: 60.5 us -> 37.1 us
    reshape x0 -> x2, local copies, waits for them, and re-layouts: none -> 20.5 us  [update_the_sites(): jnp.concatenate(lax.all_to_all(jnp.stack(jnp.split(slab_in, lax.psum(1, a...]
    all_to_all x2 -> x0, local copies, waits for them, and re-layouts: 19.3 us -> none  [per_device(): lax.all_to_all(spectrum_grad, 'row', split_axis=3, concat_axis=2, tiled=T...]
    another operation x1 -> x0, local copies, waits for them, and re-layouts: 15.1 us -> none  [per_device(): jnp.stack([(back_cos[:, 0] + back_sin[:, 1]) * inverse, (back_cos[:, 1] -...]
where the time goes in v1:
time: 486 us; the launch traced here: 480 us
  matrix products  156 us (32%)
  blocking collectives  121 us (25%)
  local copies, waits for them, and re-layouts  90.2 us (19%)
  other arithmetic  50 us (10%)
  waiting for transfers between devices  36.4 us (7%)
  between operations  14.5 us (3%)
  starting transfers between devices  12.1 us (2%)
    psum x1, blocking collectives, per_device(): coef_grad = lax.psum(coef_part, ('star', 'row'))  78.2 us
    all_to_all x1, blocking collectives, update_the_sites(): lax.all_to_all(jnp.stack(jnp.split(slab_in, lax.psum(1, axis_name='row'),...  42.6 us
    unnamed x17, local copies, waits for them, and re-layouts  37.1 us
    all_to_all x1, waiting for transfers between devices, per_device(): lax.all_to_all(column_field, 'row', split_axis=3, concat_axis=2, tiled=True)  36.3 us
    unnamed x31, other arithmetic  24.5 us
    reshape x2, local copies, waits for them, and re-layouts, update_the_sites(): jnp.concatenate(lax.all_to_all(jnp.stack(jnp.split(slab_in, lax.psum(1, a...  20.5 us
    all_to_all x2, local copies, waits for them, and re-layouts, per_device(): lax.all_to_all(column_field, 'row', split_axis=3, concat_axis=2, tiled=True)  18.2 us
    dot_general x1, matrix products, per_device(): jnp.einsum('sarc,cv->sarv', pupil_field, sin_table, preferred_element_typ...  17.6 us
  transfers between devices with their start and end apart: 2, of which 1 were waited for; matrix products, arithmetic and copies ran while one was open for 2% of the time, Pallas kernels for 0%

profile of v1, /device:TPU:1, one launch (start us, length us, event | category | flops | bytes accessed | tf_op | source)
XLA Modules:
  0.0 480.1 jit_solution(8144197037946635837)
XLA Ops:
  7.2 0.8 broadcast_in_dim.72
  8.0 0.8 broadcast_in_dim.75
  9.2 6.7 %fusion.3 = f32[12,32,1024]{2,0,1:T(8,128)S(1)} fusion(bf16[12,64]{1,0:T(8,128)(2,1)S(1)} %convolution_convert_fusion, bf16[8,8,32,1024]{3,2,1,0:T(8,128)(2,1)} %bitcast.154), kind=kOutput, calls=%fused_computation.69 | convolution fusion | flops 50331648 | bytes 5768704 | tf_op jit(solution)/shard_map/dot_general | solution.py:67
  16.0 1.3 copy-done.2
  17.3 8.7 %fusion.54 = (bf16[12,1,32,1024]{3,0,2,1:T(8,128)(2,1)S(1)}, bf16[12,1,32,1024]{3,0,2,1:T(8,128)(2,1)S(1)}) fusion(f32[12,32,1024]{2,0,1:T(8,128)S(1)} %fusion.3, f32[32,1024]{1,0:T(8,128)S(1)} %fusion.89, f32[12]{0:T(128)S(1)} %add_divide_fusion), kind=kLoop, calls=%fused_computation.127 | loop fusion | flops 1966080 | bytes 3276848 | tf_op jit(solution)/shard_map/stack | solution.py:75
  26.3 17.6 %fusion.28 = f32[12,2,32,1024]{3,2,1,0:T(8,128)S(1)} fusion(bf16[12,2,32,1024]{3,0,2,1:T(8,128)(2,1)S(1)} %pad_maximum_fusion), kind=kOutput, calls=%fused_computation.97 | convolution fusion | flops 1627389952 | bytes 4718592 | tf_op jit(solution)/shard_map/sarc,cv->sarv/dot_general | solution.py:81
  43.9 17.6 %fusion.36 = f32[12,2,32,1024]{3,2,1,0:T(8,128)S(1)} fusion(bf16[12,2,32,1024]{3,0,2,1:T(8,128)(2,1)S(1)} %pad_maximum_fusion), kind=kOutput, calls=%fused_computation.101 | convolution fusion | flops 1626341376 | bytes 4718592 | tf_op jit(solution)/shard_map/sarc,cv->sarv/dot_general | solution.py:78
  61.5 1.0 fusion.45
  62.7 11.3 %copy.43 = bf16[12,2,32,1024]{2,1,0,3:T(2,128)(2,1)} copy(bf16[12,2,32,1024]{3,2,1,0:T(8,128)(2,1)S(1)} %pad_maximum_fusion.1) | data formatting | bytes 3145728 | tf_op jit(solution)/shard_map/stack | solution.py:84
  73.9 13.8 %reshape.101 = bf16[32,2,12288]{2,1,0:T(2,128)(2,1)} reshape(bf16[1024,12,2,32]{3,2,1,0:T(2,128)(2,1)} %bitcast.153) | data formatting | bytes 3145728
  87.8 12.0 %all-to-all-start = ((bf16[32,2,12288]{2,1,0:T(2,128)(2,1)}), bf16[32,2,12288]{2,1,0:T(2,128)(2,1)S(1)}, u32[]{:S(2)}, u32[]{:S(2)}) async-start(bf16[32,2,12288]{2,1,0:T(2,128)(2,1)} %reshape.101), calls=%async_computation | async-start | bytes 3145728 | tf_op jit(solution)/shard_map/all_to_all | solution.py:87
  100.0 1.4 convert_multiply_fusion
  101.3 36.3 %all-to-all-done = bf16[32,2,12288]{2,1,0:T(2,128)(2,1)S(1)} async-done(((bf16[32,2,12288]{2,1,0:T(2,128)(2,1)}), bf16[32,2,12288]{2,1,0:T(2,128)(2,1)S(1)}, u32[]{:S(2)}, u32[]{:S(2)}) %all-to-all-start) | async-done | bytes 1572896 | tf_op jit(solution)/shard_map/all_to_all | solution.py:87
  137.7 4.6 reshape.102
  142.3 9.5 %copy.102 = bf16[12,2,32,32,32]{2,3,4,1,0:T(8,128)(2,1)} copy(bf16[12,2,32,32,32]{2,1,0,4,3:T(2,128)(2,1)} %bitcast.150) | data formatting | bytes 3145728 | tf_op jit(solution)/shard_map/all_to_all | solution.py:87
  151.8 8.8 %all_to_all.19 = bf16[12,2,1024,32]{2,3,1,0:T(8,128)(2,1)S(1)} reshape(bf16[12,2,32,32,32]{3,2,4,1,0:T(8,128)(2,1)} %bitcast.151) | data formatting | bytes 3145728 | tf_op jit(solution)/shard_map/all_to_all | solution.py:87
  160.5 17.3 %fusion.26 = f32[12,2,32,1024]{3,2,1,0:T(8,128)S(1)} fusion(bf16[12,2,1024,32]{2,3,1,0:T(8,128)(2,1)S(1)} %all_to_all.19), kind=kOutput, calls=%fused_computation.96 | convolution fusion | flops 1627389952 | bytes 4718592 | tf_op jit(solution)/shard_map/sarv,ru->savu/dot_general | solution.py:89
  177.8 17.4 %fusion.34 = f32[12,2,32,1024]{3,2,1,0:T(8,128)S(1)} fusion(bf16[12,2,1024,32]{2,3,1,0:T(8,128)(2,1)S(1)} %all_to_all.19), kind=kOutput, calls=%fused_computation.100 | convolution fusion | flops 1626341376 | bytes 4718592 | tf_op jit(solution)/shard_map/sarv,ru->savu/dot_general | solution.py:88
  195.2 1.0 fusion.43
  196.3 16.6 %fusion.24 = f32[12,2,32,1024]{3,2,1,0:T(8,128)S(1)} fusion(f32[12,1,32,1024]{3,2,1,0:T(8,128)S(1)} %get-tuple-element.15, f32[12,1,32,1024]{3,2,1,0:T(8,128)S(1)} %get-tuple-element.14, f32[12,32,1024]{2,1,0:T(8,128)S(1)} %convert_multiply_fusion), kind=kOutput, calls=%fused_computation.95 | convolution fusion | flops 1629749248 | bytes 7864320 | tf_op jit(solution)/shard_map/savu,ur->savr/dot_general | solution.py:100
  212.9 16.6 %fusion.32 = f32[12,2,32,1024]{3,2,1,0:T(8,128)S(1)} fusion(f32[12,1,32,1024]{3,2,1,0:T(8,128)S(1)} %get-tuple-element.15, f32[12,1,32,1024]{3,2,1,0:T(8,128)S(1)} %get-tuple-element.14, f32[12,32,1024]{2,1,0:T(8,128)S(1)} %convert_multiply_fusion), kind=kOutput, calls=%fused_computation.99 | convolution fusion | flops 1628700672 | bytes 7864320 | tf_op jit(solution)/shard_map/savu,ur->savr/dot_general | solution.py:97
  229.5 0.8 fusion.41
  231.0 0.8 bitcast_dynamic-update-slice_fusion.29
  231.8 0.8 bitcast_dynamic-update-slice_fusion.28
  232.6 0.8 bitcast_dynamic-update-slice_fusion.27
  233.4 0.7 bitcast_dynamic-update-slice_fusion.26
  234.2 0.8 bitcast_dynamic-update-slice_fusion.25
  235.0 0.8 bitcast_dynamic-update-slice_fusion.24
  235.8 0.8 bitcast_dynamic-update-slice_fusion.23
  236.6 0.7 bitcast_dynamic-update-slice_fusion.22
  237.3 0.8 bitcast_dynamic-update-slice_fusion.21
  238.1 0.8 bitcast_dynamic-update-slice_fusion.20
  238.9 1.0 bitcast_dynamic-update-slice_fusion.19
  240.6 0.8 bitcast_dynamic-update-slice_fusion.17
  241.4 0.8 bitcast_dynamic-update-slice_fusion.16
  242.2 0.8 bitcast_dynamic-update-slice_fusion.15
  243.0 0.7 bitcast_dynamic-update-slice_fusion.14
  243.7 0.8 bitcast_dynamic-update-slice_fusion.13
  244.6 0.8 bitcast_dynamic-update-slice_fusion.12
  245.4 0.8 bitcast_dynamic-update-slice_fusion.11
  246.2 0.7 bitcast_dynamic-update-slice_fusion.10
  246.9 0.8 bitcast_dynamic-update-slice_fusion.9
  247.7 0.8 bitcast_dynamic-update-slice_fusion.8
  248.5 0.8 bitcast_dynamic-update-slice_fusion.7
  250.0 0.8 bitcast_dynamic-update-slice_fusion.5
  250.8 0.8 bitcast_dynamic-update-slice_fusion.4
  251.6 0.8 bitcast_dynamic-update-slice_fusion.3
  252.5 0.7 bitcast_dynamic-update-slice_fusion.2
  253.2 0.8 bitcast_dynamic-update-slice_fusion.1
  254.0 0.8 bitcast_dynamic-update-slice_fusion
  254.8 0.8 fusion.88
  255.6 8.8 %reshape.103 = bf16[32,2,12288]{2,1,0:T(2,128)(2,1)S(1)} reshape(bf16[32,12,2,32,32]{4,3,2,1,0:T(8,128)(2,1)} %fusion.88) | data formatting | bytes 3145728
  264.4 42.6 %all_to_all.23 = bf16[32,2,12288]{2,1,0:T(2,128)(2,1)S(1)} all-to-all(bf16[32,2,12288]{2,1,0:T(2,128)(2,1)S(1)} %reshape.103), channel_id=1, replica_groups=mesh['star'=8,'row'=32] {'row'}, dimensions={0} | all-to-all | bytes 3145728 | tf_op jit(solution)/shard_map/all_to_all | solution.py:11
  307.0 4.6 reshape.104
  311.6 11.7 %copy.45 = bf16[12,2,32,32,32]{3,2,4,1,0:T(8,128)(2,1)} copy(bf16[12,2,32,32,32]{4,3,1,0,2:T(8,128)(2,1)} %bitcast.152) | data formatting | bytes 3145728 | tf_op jit(solution)/shard_map/reshape | solution.py:10
  323.3 8.8 %reshape.94 = bf16[12,2,1024,32]{2,3,1,0:T(8,128)(2,1)S(1)} reshape(bf16[12,2,32,32,32]{3,2,4,1,0:T(8,128)(2,1)} %copy.45) | data formatting | bytes 3145728 | tf_op jit(solution)/shard_map/reshape | solution.py:10
  332.1 17.3 %fusion.22 = f32[12,2,32,1024]{3,2,1,0:T(8,128)S(1)} fusion(bf16[12,2,1024,32]{2,3,1,0:T(8,128)(2,1)S(1)} %reshape.94), kind=kOutput, calls=%fused_computation.94 | convolution fusion | flops 1627389952 | bytes 4718592 | tf_op jit(solution)/shard_map/savr,vc->sarc/dot_general | solution.py:109
  349.4 17.2 %fusion.30 = f32[12,2,32,1024]{3,2,1,0:T(8,128)S(1)} fusion(bf16[12,2,1024,32]{2,3,1,0:T(8,128)(2,1)S(1)} %reshape.94), kind=kOutput, calls=%fused_computation.98 | convolution fusion | flops 1626341376 | bytes 4718592 | tf_op jit(solution)/shard_map/savr,vc->sarc/dot_general | solution.py:108
  366.6 1.1 fusion.128
  368.2 11.1 %fusion.19 = bf16[12,32,1024]{2,0,1:T(8,128)(2,1)S(1)} fusion(f32[12,1,32,1024]{3,2,1,0:T(8,128)S(1)} %get-tuple-element.24, f32[12,1,32,1024]{3,2,1,0:T(8,128)S(1)} %get-tuple-element.19, f32[12,1,32,1024]{3,2,1,0:T(8,128)S(1)} %get-tuple-element.25, f32[12,1,32,1024]{3,2,1,0:T(8,128)S(1)} %get-tuple-element.18, f32[12,32,1024]{2,0,1:T(8,128)S(1)} %copy-done.3, ...), kind=kLoop, calls=%fused_computation.90 | loop fusion | flops 3538944 | bytes 8781872 | tf_op jit(solution)/shard_map/convert_element_type | solution.py:114
  380.4 4.5 fusion.130
  385.0 6.8 %fusion.51 = f32[12,64]{1,0:T(8,128)S(1)} fusion(bf16[12,32,1024]{2,0,1:T(8,128)(2,1)S(1)} %fusion.19, bf16[64,32,1024]{2,1,0:T(8,128)(2,1)} %param.6), kind=kOutput, calls=%fused_computation.125 | convolution fusion | flops 50332416 | bytes 4983808 | tf_op jit(solution)/shard_map/dot_general | solution.py:117
  392.0 78.2 %psum.7 = f32[64,64]{1,0:T(8,128)} all-reduce(f32[64,64]{1,0:T(8,128)S(1)} %fusion.90), channel_id=1, replica_groups=mesh['star'=8,'row'=32] {'star','row'}, use_global_device_ids=true, to_apply=%region_4.5 | all-reduce | flops 4096 | bytes 32768 | tf_op jit(solution)/shard_map/psum | solution.py:126
  470.2 2.8 copy.52
  (30 shorter events, 5.1 us)
Async XLA Ops:
  7.2 1.8 copy-start
  16.0 1.3 copy-start.2
  73.9 25.9 %copy-start.4 = (s32[8]{0:T(128)S(1)}, s32[8]{0:T(128)}, u32[]{:S(2)}) copy-start(s32[8]{0:T(128)} %param.8) | copy-start | bytes 100
  87.8 49.9 %all-to-all-start = ((bf16[32,2,12288]{2,1,0:T(2,128)(2,1)}), bf16[32,2,12288]{2,1,0:T(2,128)(2,1)S(1)}, u32[]{:S(2)}, u32[]{:S(2)}) async-start(bf16[32,2,12288]{2,1,0:T(2,128)(2,1)} %reshape.101), calls=%async_computation | async-start | bytes 3145728 | tf_op jit(solution)/shard_map/all_to_all | solution.py:87
  99.8 370.4 %reduce-scatter.2.cloned.1.call-start = ((), (), s32[]{:S(2)}) async-start(), calls=%async_computation.3 | async-start | bytes 9437184 | tf_op jit(solution)/shard_map/reduce_scatter | solution.py:128
  366.6 1.6 copy-start.3
  385.0 88.1 %copy-start.1 = (bf16[64,64]{1,0:T(8,128)(2,1)S(1)}, bf16[64,64]{1,0:T(8,128)(2,1)}, u32[]{:S(2)}) copy-start(bf16[64,64]{1,0:T(8,128)(2,1)} %param.7) | copy-start | bytes 24580
Sparse Core Ops, SparseCore 0:
  385.1 54.6 reduce-scatter.1
